TPU v7x, 256 devices: a whole 4x4x8 slice. The times are simulated.
256 devices in a mesh: tm: 8 (over y, core), head: 32 (over z, x).
Axes of the slice: x: 4, y: 4, z: 8, core: 2. Of those that a mesh axis runs over, the one named last changes fastest.
Arguments:
- tokens: bfloat16 [4096, 5120], P('tm'), may hold values from -24 to 24
- w_query: bfloat16 [5120, 4096], P(None, 'head'), may hold values from -0.078125 to 0.078125
- w_key: bfloat16 [5120, 4096], P(None, 'head'), may hold values from -0.078125 to 0.078125
- w_value: bfloat16 [5120, 4096], P(None, 'head'), may hold values from -0.078125 to 0.078125
- w_out: bfloat16 [4096, 5120], P('head'), may hold values from -0.09375 to 0.09375
- out_grad: bfloat16 [4096, 5120], P('tm'), may hold values from -6 to 6
- frame_lists: int32 [8, 8], replicated, may hold values from 0 to 1, as said below
Outputs:
- token_grad: bfloat16 [4096, 5120], P(('tm', 'head'))
- query_grad: bfloat16 [5120, 4096], P('tm', 'head')
- key_grad: bfloat16 [5120, 4096], P('tm', 'head')
- value_grad: bfloat16 [5120, 4096], P('tm', 'head')
- out_weight_grad: bfloat16 [4096, 5120], P('head', 'tm')
Inputs may be any that keep to these rules, and one draw needn't show every extreme that they name: `frame_lists`: entries with j >= i are 0; entry (i, i - 1) is 1 for every group i > 0.
All inputs are finite; a program needn't handle non-finite values.
Results may differ from a plain program's by a relative error of at most 0.02.
The roundings to bfloat16 on the way count: a program that leaves them out, or rounds other values in their place, can miss the bound.
Values may be sent and summed in bfloat16 or wider, within the bound.
A program may use at most 128 MiB of HBM per device.

v0:
```python
import jax
import jax.numpy as jnp
from jax import lax
from jax.sharding import PartitionSpec as P


def contract_rows(left, right):
    return lax.dot_general(
        left, right, (((0,), (0,)), ((), ())), preferred_element_type=jnp.float32
    )


def contract_cols(left, right):
    return lax.dot_general(
        left, right, (((1,), (1,)), ((), ())), preferred_element_type=jnp.float32
    )


def local(tokens, w_query, w_key, w_value, w_out, out_grad, frame_lists):
    width = w_query.shape[1]
    scale = 1.0 / width**0.5
    rows = tokens.shape[0]
    groups = lax.axis_size("tm")
    mine = lax.axis_index("tm")
    query = jnp.dot(tokens, w_query, preferred_element_type=jnp.float32).astype(jnp.bfloat16)
    keys = jnp.dot(tokens, w_key, preferred_element_type=jnp.float32).astype(jnp.bfloat16)
    values = jnp.dot(tokens, w_value, preferred_element_type=jnp.float32).astype(jnp.bfloat16)
    d_attn = contract_cols(out_grad, w_out).astype(jnp.bfloat16)
    my_list = lax.dynamic_slice_in_dim(frame_lists, mine, 1, 0)[0]
    key_all, value_all = (
        lax.all_gather(keys, "tm", axis=0, tiled=True),
        lax.all_gather(values, "tm", axis=0, tiled=True),
    )
    order = jnp.arange(groups, dtype=jnp.int32)
    allowed = (order == mine) | (my_list == 1) & (order < mine)
    key_mask = jnp.repeat(allowed, rows)[None, :]
    scores = contract_cols(query, key_all) * scale
    scores = jnp.where(key_mask, scores, jnp.float32(-1e30))
    top = jnp.max(scores, axis=1, keepdims=True)
    expd = jnp.exp(scores - top)
    probs = expd / jnp.sum(expd, axis=1, keepdims=True)
    probs_b = probs.astype(jnp.bfloat16)
    attn = jnp.dot(probs_b, value_all, preferred_element_type=jnp.float32).astype(jnp.bfloat16)
    dprobs = contract_cols(d_attn, value_all)
    delta = jnp.sum(probs * dprobs, axis=1, keepdims=True)
    dscore = (probs * (dprobs - delta) * scale).astype(jnp.bfloat16)
    dquery = jnp.dot(dscore, key_all, preferred_element_type=jnp.float32).astype(jnp.bfloat16)
    cache_terms = jnp.concatenate(
        [contract_rows(dscore, query), contract_rows(probs_b, d_attn)], axis=1
    )
    summed = lax.psum_scatter(
        cache_terms.astype(jnp.bfloat16), "tm", scatter_dimension=0, tiled=True
    ).astype(jnp.float32)
    dkey = summed[:, :width].astype(jnp.bfloat16)
    dvalue = summed[:, width:].astype(jnp.bfloat16)
    weights_sum = lax.psum_scatter(
        jnp.concatenate(
            [
                contract_rows(tokens, dquery),
                contract_rows(tokens, dkey),
                contract_rows(tokens, dvalue),
                contract_rows(out_grad, attn),
            ],
            axis=1,
        ).astype(jnp.bfloat16),
        "tm",
        scatter_dimension=0,
        tiled=True,
    ).astype(jnp.float32)
    query_grad = weights_sum[:, :width].astype(jnp.bfloat16)
    key_grad = weights_sum[:, width : 2 * width].astype(jnp.bfloat16)
    value_grad = weights_sum[:, 2 * width : 3 * width].astype(jnp.bfloat16)
    out_weight_grad = weights_sum[:, 3 * width :].T.astype(jnp.bfloat16)
    token_grad = lax.psum_scatter(
        (
            contract_cols(dquery, w_query)
            + contract_cols(dkey, w_key)
            + contract_cols(dvalue, w_value)
        ).astype(jnp.bfloat16),
        "head",
        scatter_dimension=0,
        tiled=True,
    )
    return (token_grad, query_grad, key_grad, value_grad, out_weight_grad)


def solution(mesh):
    in_specs = (
        P("tm", None),
        P(None, "head"),
        P(None, "head"),
        P(None, "head"),
        P("head", None),
        P("tm", None),
        P(),
    )
    out_specs = (
        P(("tm", "head"), None),
        P("tm", "head"),
        P("tm", "head"),
        P("tm", "head"),
        P("head", "tm"),
    )
    return jax.shard_map(local, mesh=mesh, in_specs=in_specs, out_specs=out_specs, check_vma=False)
```

profile of v0, /device:TPU:8, one launch (start us, length us, event | category | flops | bytes accessed | tf_op | source)
XLA Modules:
  0.0 424.9 jit_solution(9849481897770291235)
XLA Ops:
  7.2 0.0 copy-start
  7.2 0.0 copy-start.7
  7.2 0.0 all-gather.3.cloned.1.call-start
  7.2 5.2 %convolution_convert_fusion.9 = bf16[512,128]{1,0:T(8,128)(2,1)} fusion(bf16[512,5120]{1,0:T(8,128)(2,1)} %param.7, bf16[5120,128]{1,0:T(8,128)(2,1)} %param.9), kind=kOutput, calls=%fused_computation.26 | convolution fusion | flops 671154176 | bytes 6684672 | tf_op jit(solution)/shard_map/dot_general | solution.py:26
  12.4 0.0 all-gather.3.cloned.1.call-update
  12.5 0.0 all-gather.5.cloned.1.call-start
  12.5 0.0 copy-done.7
  12.5 4.7 %convolution_convert_fusion.7 = bf16[512,128]{1,0:T(8,128)(2,1)} fusion(bf16[512,5120]{1,0:T(8,128)(2,1)} %param.7, bf16[5120,128]{1,0:T(8,128)(2,1)S(1)} %copy-done.7), kind=kOutput, calls=%fused_computation.24 | convolution fusion | flops 671154176 | bytes 6684672 | tf_op jit(solution)/shard_map/dot_general | solution.py:27
  17.2 0.0 copy-start.9
  17.2 0.0 all-gather.5.cloned.1.call-update
  17.2 0.0 reduce-scatter.6.cloned.1.call-start
  17.3 0.8 fusion.20
  18.0 0.1 broadcast_bitcast_fusion
  18.1 0.0 copy-done
  18.1 4.0 convolution_convert_fusion.10
  22.1 0.0 copy-done.9
  22.2 4.0 convolution_convert_fusion.8
  26.2 13.5 %all-gather.3.cloned.1.call-done = bf16[4096,128]{1,0:T(8,128)(2,1)} async-done(((bf16[512,128]{1,0:T(8,128)(2,1)}), bf16[4096,128]{1,0:T(8,128)(2,1)}) %all-gather.3.cloned.1.call-update) | async-done | bytes 1048592 | tf_op jit(solution)/shard_map/all_gather | solution.py:31
  39.7 2.7 fusion
  42.5 0.0 copy-start.2
  42.5 3.2 copy-done.2
  45.7 2.2 fusion.2
  47.9 20.2 %all-gather.5.cloned.1.call-done = bf16[4096,128]{1,0:T(8,128)(2,1)} async-done(((bf16[512,128]{1,0:T(8,128)(2,1)}), bf16[4096,128]{1,0:T(8,128)(2,1)}) %all-gather.5.cloned.1.call-update) | async-done | bytes 1048592 | tf_op jit(solution)/shard_map/all_gather | solution.py:32
  68.0 7.4 %multiply_reduce_fusion = (f32[512]{0:T(512)S(1)}, f32[512,4096]{1,0:T(8,128)S(1)}, f32[512,4096]{1,0:T(8,128)}) fusion(f32[512]{0:T(512)S(1)} %fusion.2, f32[512]{0:T(512)S(1)} %get-tuple-element.21, f32[512,4096]{1,0:T(8,128)} %copy-done.2, pred[4096]{0:T(1024)(128)(4,1)S(1)} %bitcast.47, bf16[512,128]{1,0:T(8,128)(2,1)S(1)} %convolution_convert_fusion.8, ...), kind=kOutput, calls=%fused_computation.2 | convolution fusion | flops 549453312 | bytes 26355712 | tf_op jit(solution)/shard_map/dot_general | solution.py:14
  75.4 0.0 copy-start.1
  75.5 0.8 convolution_convert_fusion.4
  76.2 2.5 copy-done.1
  78.7 8.0 %multiply_convert_fusion = bf16[512,4096]{1,0:T(8,128)(2,1)S(1)} fusion(f32[512,4096]{1,0:T(8,128)} %copy-done.1, f32[512,4096]{1,0:T(8,128)} %get-tuple-element.23, f32[512]{0:T(512)S(1)} %get-tuple-element.15), kind=kLoop, calls=%fused_computation.1 | loop fusion | flops 8388608 | bytes 20973568 | tf_op jit(solution)/shard_map/convert_element_type | solution.py:46
  86.7 0.0 copy-start.3
  86.7 2.0 copy-done.3
  88.7 0.8 convolution_convert_fusion.5
  89.5 1.5 pad_maximum_fusion.1
  90.9 0.0 reduce-scatter.6.cloned.1.call-update
  91.0 0.2 reduce-scatter.10.cloned.1.call-start
  91.2 3.7 convolution_convert_fusion.6
  94.9 3.4 fusion.3
  98.3 9.7 %fusion.6 = bf16[5120,128]{0,1:T(8,128)(2,1)} fusion(bf16[512,5120]{1,0:T(8,128)(2,1)} %param.12, bf16[4096,128]{1,0:T(8,128)(2,1)} %all-gather.5.cloned.1.call-done, f32[512,4096]{1,0:T(8,128)} %copy-done.1), kind=kOutput, calls=%fused_computation.15 | convolution fusion | flops 1210777600 | bytes 15990784 | tf_op jit(solution)/shard_map/dot_general | solution.py:8
  108.0 17.6 %reduce-scatter.6.cloned.1.call-done = bf16[512,256]{0,1:T(8,128)(2,1)} async-done(((bf16[4096,256]{0,1:T(8,128)(2,1)}), bf16[512,256]{0,1:T(8,128)(2,1)}) %reduce-scatter.6.cloned.1.call-update) | async-done | bytes 262160 | tf_op jit(solution)/shard_map/reduce_scatter | solution.py:51
  125.6 0.0 copy-start.5
  125.6 3.5 fusion.4
  129.1 0.0 copy-done.5
  129.1 0.0 copy-start.4
  129.1 3.4 fusion.5
  132.5 0.0 copy-done.4
  132.6 3.5 pad_maximum_fusion
  136.1 7.9 %copy.18 = bf16[5120,512]{1,0:T(8,128)(2,1)} copy(bf16[5120,512]{0,1:T(8,128)(2,1)} %pad_maximum_fusion) | data formatting | bytes 10485760
  144.0 0.0 reduce-scatter.10.cloned.1.call-update
  144.0 0.0 copy-start.6
  144.0 0.0 reduce-scatter.8.cloned.1.call-start
  144.1 1.5 fusion.23
  145.6 0.0 copy-done.6
  145.6 0.0 copy-start.8
  145.6 5.5 %fusion.18 = f32[512,5120]{1,0:T(8,128)} fusion(bf16[5120,128]{1,0:T(8,128)(2,1)S(1)} %copy-done.6, bf16[512,256]{0,1:T(8,128)(2,1)S(1)} %copy-done.5), kind=kOutput, calls=%fused_computation.32 | convolution fusion | flops 671088640 | bytes 11927552 | tf_op jit(solution)/shard_map/dot_general | solution.py:14
  151.2 0.0 copy-done.8
  151.2 8.2 %add_convert_fusion = bf16[512,5120]{1,0:T(8,128)(2,1)} fusion(f32[512,5120]{1,0:T(8,128)S(1)} %fusion.23, f32[512,5120]{1,0:T(8,128)} %fusion.18, bf16[5120,128]{1,0:T(8,128)(2,1)S(1)} %copy-done.8, bf16[512,256]{0,1:T(8,128)(2,1)S(1)} %copy-done.5), kind=kOutput, calls=%fused_computation | convolution fusion | flops 678952960 | bytes 27656192 | tf_op jit(solution)/shard_map/dot_general | solution.py:14
  159.3 0.0 reduce-scatter.8.cloned.1.call-update
  159.4 25.7 %reduce-scatter.10.cloned.1.call-done = bf16[640,512]{1,0:T(8,128)(2,1)} async-done(((bf16[5120,512]{1,0:T(8,128)(2,1)}), bf16[640,512]{1,0:T(8,128)(2,1)}) %reduce-scatter.10.cloned.1.call-update) | async-done | bytes 655376
  185.1 2.0 fusion.22
  187.0 0.8 copy.23
  187.8 230.5 %reduce-scatter.8.cloned.1.call-done = bf16[16,5120]{1,0:T(8,128)(2,1)} async-done(((bf16[512,5120]{1,0:T(8,128)(2,1)}), bf16[16,5120]{1,0:T(8,128)(2,1)}) %reduce-scatter.8.cloned.1.call-update) | async-done | bytes 163856 | tf_op jit(solution)/shard_map/reduce_scatter | solution.py:74
  (1 shorter events, 0.0 us)
Async XLA Ops:
  7.2 11.0 %copy-start = (bf16[5120,128]{1,0:T(8,128)(2,1)S(1)}, bf16[5120,128]{1,0:T(8,128)(2,1)}, u32[]{:S(2)}) copy-start(bf16[5120,128]{1,0:T(8,128)(2,1)} %param.8) | copy-start | bytes 3932164
  7.2 5.3 %copy-start.7 = (bf16[5120,128]{1,0:T(8,128)(2,1)S(1)}, bf16[5120,128]{1,0:T(8,128)(2,1)}, u32[]{:S(2)}) copy-start(bf16[5120,128]{1,0:T(8,128)(2,1)} %param.10) | copy-start | bytes 3932164
  7.2 32.6 %all-gather.3.cloned.1.call-start = ((), (), s32[]{:S(2)}) async-start(), calls=%async_computation.3 | async-start | bytes 1179648 | tf_op jit(solution)/shard_map/all_gather | solution.py:31
  12.5 55.6 %all-gather.5.cloned.1.call-start = ((), (), s32[]{:S(2)}) async-start(), calls=%async_computation.4 | async-start | bytes 1179648 | tf_op jit(solution)/shard_map/all_gather | solution.py:32
  17.2 5.0 %copy-start.9 = (bf16[128,5120]{1,0:T(8,128)(2,1)S(1)}, bf16[128,5120]{1,0:T(8,128)(2,1)}, u32[]{:S(2)}) copy-start(bf16[128,5120]{1,0:T(8,128)(2,1)} %param.11) | copy-start | bytes 3932164
  17.2 108.4 %reduce-scatter.6.cloned.1.call-start = ((), (), s32[]{:S(2)}) async-start(), calls=%async_computation.5 | async-start | bytes 2359296 | tf_op jit(solution)/shard_map/reduce_scatter | solution.py:51
  42.5 3.2 copy-start.2
  75.4 3.2 copy-start.1
  86.7 2.0 copy-start.3
  91.0 94.1 %reduce-scatter.10.cloned.1.call-start = ((), (), s32[]{:S(2)}) async-start(), calls=%async_computation.7 | async-start | bytes 5898240
  125.6 3.5 copy-start.5
  129.1 3.5 copy-start.4
  144.0 1.6 copy-start.6
  144.0 274.3 %reduce-scatter.8.cloned.1.call-start = ((), (), s32[]{:S(2)}) async-start(), calls=%async_computation.6 | async-start | bytes 5406720 | tf_op jit(solution)/shard_map/reduce_scatter | solution.py:74
  145.6 5.5 %copy-start.8 = (bf16[5120,128]{1,0:T(8,128)(2,1)S(1)}, bf16[5120,128]{1,0:T(8,128)(2,1)}, u32[]{:S(2)}) copy-start(bf16[5120,128]{1,0:T(8,128)(2,1)} %param.10) | copy-start | bytes 3932164
Sparse Core Ops, SparseCore 0:
  12.6 27.1 all-gather.2
  42.2 25.7 all-gather.4
  91.1 34.4 reduce-scatter.5
  144.1 40.9 reduce-scatter.9
  189.5 228.8 reduce-scatter.7
where the time goes:
time: 425 us
  waiting for transfers between devices  308 us (72%)
  matrix products  68.5 us (16%)
  local copies, waits for them, and re-layouts  18.5 us (4%)
  other arithmetic  16 us (4%)
  between operations  14 us (3%)
    reduce_scatter x1, waiting for transfers between devices, local(): lax.psum_scatter((contract_cols(dquery, w_query) + contract_cols(dkey, w_...  231 us
    dot_general x6, matrix products, contract_cols(): lax.dot_general(left, right, (((1,), (1,)), ((), ())), preferred_element_...  29.4 us
    unnamed x6, waiting for transfers between devices  25.8 us
    dot_general x6, matrix products, contract_rows(): lax.dot_general(left, right, (((0,), (0,)), ((), ())), preferred_element_...  21.5 us
    all_gather x1, waiting for transfers between devices, local(): lax.all_gather(values, 'tm', axis=0, tiled=True)  20.2 us
    reduce_scatter x1, waiting for transfers between devices, local(): lax.psum_scatter(cache_terms.astype(jnp.bfloat16), 'tm', scatter_dimensio...  17.6 us
    unnamed x24, local copies, waits for them, and re-layouts  16.5 us
    all_gather x1, waiting for transfers between devices, local(): lax.all_gather(keys, 'tm', axis=0, tiled=True)  13.5 us
  transfers between devices with their start and end apart: 5, of which 5 were waited for; matrix products, arithmetic and copies ran while one was open for 13% of the time, Pallas kernels for 0%

commit v1 on v0

--- a/solution.py
+++ b/solution.py
@@ -2,6 +2,28 @@
 import jax.numpy as jnp
 from jax import lax
 from jax.sharding import PartitionSpec as P
+
+
+def in_order(blocks, dim):
+    lengths = list(blocks.shape[1:])
+    lengths[dim] *= blocks.shape[0]
+    return jnp.moveaxis(blocks, 0, dim).reshape(lengths)
+
+
+def gather_around(x, axis, dim):
+    size = lax.axis_size(axis)
+    pairs = [(i, (i + 1) % size) for i in range(size)]
+    back = [(b, a) for a, b in pairs]
+    lower, upper = ([], [])
+    for step in range(size - 1):
+        if step % 2 == 0:
+            lower.append(lax.ppermute(lower[-1] if lower else x, axis, pairs))
+        else:
+            upper.append(lax.ppermute(upper[-1] if upper else x, axis, back))
+    blocks = jnp.stack([*lower[::-1], x, *upper])
+    shift = lax.axis_index(axis) - len(lower)
+    blocks = blocks[(jnp.arange(size) - shift) % size]
+    return in_order(blocks, dim)
 
 
 def contract_rows(left, right):
@@ -29,7 +51,7 @@
     my_list = lax.dynamic_slice_in_dim(frame_lists, mine, 1, 0)[0]
     key_all, value_all = (
         lax.all_gather(keys, "tm", axis=0, tiled=True),
-        lax.all_gather(values, "tm", axis=0, tiled=True),
+        gather_around(values, "tm", 0),
     )
     order = jnp.arange(groups, dtype=jnp.int32)
     allowed = (order == mine) | (my_list == 1) & (order < mine)

time: 425 us -> 404 us (0.951)
  waiting for transfers between devices: 308 us -> 285 us
  starting transfers between devices: 0.39 us -> 6.12 us
  matrix products: 68.5 us -> 63.9 us
    all_gather x1 -> x0, waiting for transfers between devices: 20.2 us -> none  [local(): lax.all_gather(values, 'tm', axis=0, tiled=True)]
    all_gather x1, waiting for transfers between devices: 13.5 us -> 5.61 us  [local(): lax.all_gather(keys, 'tm', axis=0, tiled=True)]
    ppermute x0 -> x7, waiting for transfers between devices: none -> 5.78 us  [the longest x4 5.77 us: gather_around(): lower.append(lax.ppermute(lower[-1] if lower else x, axis, pairs))]
    ppermute x0 -> x7, starting transfers between devices: none -> 5.56 us  [the longest x3 3.34 us: gather_around(): upper.append(lax.ppermute(upper[-1] if upper else x, axis, back))]
    unnamed x24 -> x41, local copies, waits for them, and re-layouts: 16.5 us -> 15.3 us
    unnamed x6 -> x5, waiting for transfers between devices: 25.8 us -> 25.8 us
  transfers between devices with their start and end apart: 5 -> 11, of which waited for: 5 -> 6; matrix products, arithmetic and copies ran while one was open for 13% -> 12% of each run, Pallas kernels for 0% -> 0%
where the time goes in v1:
time: 404 us; the launch traced here: 403 us
  waiting for transfers between devices  285 us (71%)
  matrix products  63.9 us (16%)
  local copies, waits for them, and re-layouts  18 us (4%)
  other arithmetic  15.9 us (4%)
  between operations  14.1 us (3%)
  starting transfers between devices  6.12 us (2%)
    reduce_scatter x1, waiting for transfers between devices, local(): lax.psum_scatter((contract_cols(dquery, w_query) + contract_cols(dkey, w_...  231 us
    dot_general x6, matrix products, contract_cols(): lax.dot_general(left, right, (((1,), (1,)), ((), ())), preferred_element_...  27.9 us
    unnamed x5, waiting for transfers between devices  25.8 us
    dot_general x6, matrix products, contract_rows(): lax.dot_general(left, right, (((0,), (0,)), ((), ())), preferred_element_...  21.5 us
    reduce_scatter x1, waiting for transfers between devices, local(): lax.psum_scatter(cache_terms.astype(jnp.bfloat16), 'tm', scatter_dimensio...  17.2 us
    unnamed x41, local copies, waits for them, and re-layouts  15.3 us
  transfers between devices with their start and end apart: 11, of which 6 were waited for; matrix products, arithmetic and copies ran while one was open for 12% of the time, Pallas kernels for 0%

profile of v1, /device:TPU:8, one launch (start us, length us, event | category | flops | bytes accessed | tf_op | source)
XLA Modules:
  0.0 403.1 jit_solution(17717103811741951310)
XLA Ops:
  7.2 0.0 copy-start
  7.2 0.0 copy-start.7
  7.2 0.0 all-gather.2.cloned.1.call-start
  7.2 0.0 copy-start.2
  7.2 4.5 %convolution_convert_fusion.7 = bf16[512,128]{1,0:T(8,128)(2,1)S(1)} fusion(bf16[512,5120]{1,0:T(8,128)(2,1)} %param.7, bf16[5120,128]{1,0:T(8,128)(2,1)} %param.10), kind=kOutput, calls=%fused_computation.25 | convolution fusion | flops 671154176 | bytes 6684672 | tf_op jit(solution)/shard_map/dot_general | solution.py:49
  11.8 0.0 copy-start.11
  11.8 0.0 collective-permute-start.4
  11.8 0.5 collective-permute-start
  12.3 2.2 convolution_convert_fusion.9
  14.5 0.0 all-gather.2.cloned.1.call-update
  14.5 0.2 reduce-scatter.6.cloned.1.call-start
  14.8 4.0 convolution_convert_fusion.10
  18.8 0.0 collective-permute-done
  18.8 0.0 copy-start.14
  18.8 0.0 copy-start.12
  18.8 1.2 collective-permute-start.1
  20.1 5.0 %convolution_convert_fusion.8 = bf16[512,128]{1,0:T(8,128)(2,1)} fusion(bf16[512,5120]{1,0:T(8,128)(2,1)} %param.12, bf16[128,5120]{1,0:T(8,128)(2,1)} %param.11), kind=kOutput, calls=%fused_computation.26 | convolution fusion | flops 671154176 | bytes 6684672 | tf_op jit(solution)/shard_map/dot_general | solution.py:36
  25.1 0.7 fusion.20
  25.8 0.0 collective-permute-done.1
  25.8 0.5 collective-permute-start.2
  26.3 0.1 broadcast_bitcast_fusion
  26.4 0.0 collective-permute-done.4
  26.4 1.3 collective-permute-start.5
  27.6 2.6 collective-permute-done.2
  30.2 0.0 collective-permute-start.3
  30.3 0.0 collective-permute-done.5
  30.3 2.1 collective-permute-start.6
  32.3 3.2 collective-permute-done.3
  35.6 0.9 bitcast_dynamic-update-slice_fusion.4
  36.6 0.9 bitcast_dynamic-update-slice_fusion.2
  37.5 0.0 collective-permute-done.6
  37.6 0.7 gather_fusion
  38.3 5.6 %all-gather.2.cloned.1.call-done = bf16[4096,128]{1,0:T(8,128)(2,1)} async-done(((bf16[512,128]{1,0:T(8,128)(2,1)}), bf16[4096,128]{1,0:T(8,128)(2,1)}) %all-gather.2.cloned.1.call-update) | async-done | bytes 1048592 | tf_op jit(solution)/shard_map/all_gather | solution.py:53
  43.9 2.7 fusion
  46.7 2.2 fusion.2
  48.8 4.9 %multiply_reduce_fusion = (f32[512]{0:T(512)S(1)}, f32[512,4096]{1,0:T(8,128)S(1)}, f32[512,4096]{1,0:T(8,128)}) fusion(f32[512]{0:T(512)S(1)} %fusion.2, f32[512]{0:T(512)S(1)} %get-tuple-element.21, f32[512,4096]{1,0:T(8,128)S(1)} %get-tuple-element.22, pred[4096]{0:T(1024)(128)(4,1)S(1)} %bitcast.68, bf16[512,128]{1,0:T(8,128)(2,1)S(1)} %copy-done.10, ...), kind=kOutput, calls=%fused_computation.3 | convolution fusion | flops 549453312 | bytes 26355712 | tf_op jit(solution)/shard_map/dot_general | solution.py:36
  53.7 0.8 convolution_convert_fusion.4
  54.5 2.5 copy-done.1
  57.0 8.0 %multiply_convert_fusion = bf16[512,4096]{1,0:T(8,128)(2,1)S(1)} fusion(f32[512,4096]{1,0:T(8,128)} %copy-done.1, f32[512,4096]{1,0:T(8,128)} %get-tuple-element.23, f32[512]{0:T(512)S(1)} %get-tuple-element.15), kind=kLoop, calls=%fused_computation.2 | loop fusion | flops 8388608 | bytes 20973568 | tf_op jit(solution)/shard_map/convert_element_type | solution.py:68
  65.0 2.0 copy-done.3
  67.0 0.8 convolution_convert_fusion.5
  67.8 1.5 pad_maximum_fusion.1
  69.3 0.0 reduce-scatter.6.cloned.1.call-update
  69.3 0.3 reduce-scatter.10.cloned.1.call-start
  69.6 3.7 convolution_convert_fusion.6
  73.3 3.4 fusion.3
  76.7 9.7 %fusion.6 = bf16[5120,128]{0,1:T(8,128)(2,1)} fusion(bf16[512,5120]{1,0:T(8,128)(2,1)} %param.12, bf16[4096,128]{1,0:T(8,128)(2,1)} %bitcast.64, f32[512,4096]{1,0:T(8,128)} %copy-done.1), kind=kOutput, calls=%fused_computation.16 | convolution fusion | flops 1210777600 | bytes 15990784 | tf_op jit(solution)/shard_map/dot_general | solution.py:30
  86.4 17.2 %reduce-scatter.6.cloned.1.call-done = bf16[512,256]{0,1:T(8,128)(2,1)} async-done(((bf16[4096,256]{0,1:T(8,128)(2,1)}), bf16[512,256]{0,1:T(8,128)(2,1)}) %reduce-scatter.6.cloned.1.call-update) | async-done | bytes 262160 | tf_op jit(solution)/shard_map/reduce_scatter | solution.py:73
  103.6 3.5 fusion.4
  107.1 3.4 fusion.5
  110.5 3.5 pad_maximum_fusion
  114.0 8.0 %copy.18 = bf16[5120,512]{1,0:T(8,128)(2,1)} copy(bf16[5120,512]{0,1:T(8,128)(2,1)} %pad_maximum_fusion) | data formatting | bytes 10485760
  122.0 0.0 reduce-scatter.10.cloned.1.call-update
  122.0 0.0 copy-start.8
  122.0 0.0 reduce-scatter.8.cloned.1.call-start
  122.1 1.5 fusion.25
  123.6 0.0 copy-start.9
  123.6 5.6 %fusion.18 = f32[512,5120]{1,0:T(8,128)} fusion(bf16[5120,128]{1,0:T(8,128)(2,1)S(1)} %copy-done.8, bf16[512,256]{0,1:T(8,128)(2,1)S(1)} %copy-done.6), kind=kOutput, calls=%fused_computation.41 | convolution fusion | flops 671088640 | bytes 11927552 | tf_op jit(solution)/shard_map/dot_general | solution.py:36
  129.2 8.2 %add_convert_fusion = bf16[512,5120]{1,0:T(8,128)(2,1)} fusion(f32[512,5120]{1,0:T(8,128)S(1)} %fusion.25, f32[512,5120]{1,0:T(8,128)} %fusion.18, bf16[5120,128]{1,0:T(8,128)(2,1)S(1)} %copy-done.9, bf16[512,256]{0,1:T(8,128)(2,1)S(1)} %copy-done.6), kind=kOutput, calls=%fused_computation.1 | convolution fusion | flops 678952960 | bytes 27656192 | tf_op jit(solution)/shard_map/dot_general | solution.py:36
  137.4 0.0 reduce-scatter.8.cloned.1.call-update
  137.4 25.7 %reduce-scatter.10.cloned.1.call-done = bf16[640,512]{1,0:T(8,128)(2,1)} async-done(((bf16[5120,512]{1,0:T(8,128)(2,1)}), bf16[640,512]{1,0:T(8,128)(2,1)}) %reduce-scatter.10.cloned.1.call-update) | async-done | bytes 655376
  163.1 2.0 fusion.24
  165.0 0.8 copy.23
  165.8 230.7 %reduce-scatter.8.cloned.1.call-done = bf16[16,5120]{1,0:T(8,128)(2,1)} async-done(((bf16[512,5120]{1,0:T(8,128)(2,1)}), bf16[16,5120]{1,0:T(8,128)(2,1)}) %reduce-scatter.8.cloned.1.call-update) | async-done | bytes 163856 | tf_op jit(solution)/shard_map/reduce_scatter | solution.py:96
  (29 shorter events, 0.2 us)
Async XLA Ops:
  7.2 7.6 %copy-start = (bf16[5120,128]{1,0:T(8,128)(2,1)S(1)}, bf16[5120,128]{1,0:T(8,128)(2,1)}, u32[]{:S(2)}) copy-start(bf16[5120,128]{1,0:T(8,128)(2,1)} %param.8) | copy-start | bytes 3932164
  7.2 5.1 %copy-start.7 = (bf16[5120,128]{1,0:T(8,128)(2,1)S(1)}, bf16[5120,128]{1,0:T(8,128)(2,1)}, u32[]{:S(2)}) copy-start(bf16[5120,128]{1,0:T(8,128)(2,1)} %param.9) | copy-start | bytes 3932164
  7.2 36.7 %all-gather.2.cloned.1.call-start = ((), (), s32[]{:S(2)}) async-start(), calls=%async_computation.3 | async-start | bytes 1179648 | tf_op jit(solution)/shard_map/all_gather | solution.py:53
  7.2 5.1 %copy-start.2 = (bf16[512,5120]{1,0:T(8,128)(2,1)S(1)}, bf16[512,5120]{1,0:T(8,128)(2,1)}, u32[]{:S(2)}) copy-start(bf16[512,5120]{1,0:T(8,128)(2,1)} %param.7) | copy-start | bytes 15728644
  11.8 7.0 %copy-start.11 = (bf16[512,128]{1,0:T(8,128)(2,1)}, bf16[512,128]{1,0:T(8,128)(2,1)S(1)}, u32[]{:S(2)}) copy-start(bf16[512,128]{1,0:T(8,128)(2,1)S(1)} %convolution_convert_fusion.7) | copy-start | bytes 393220
  11.8 14.6 %collective-permute-start.4 = (bf16[512,128]{1,0:T(8,128)(2,1)S(1)}, bf16[512,128]{1,0:T(8,128)(2,1)S(1)}, u32[]{:S(2)}, u32[]{:S(2)}) collective-permute-start(bf16[512,128]{1,0:T(8,128)(2,1)S(1)} %convolution_convert_fusion.7), channel_id=1, source_target_pairs={{32,0},{64,32},{96,64},{128,96},{160,128},{192,160},{224,192},{0,2... | collective-permute-start | bytes 393224 | tf_op jit(solution)/shard_map/ppermute | solution.py:22
  11.8 7.0 %collective-permute-start = (bf16[512,128]{1,0:T(8,128)(2,1)S(1)}, bf16[512,128]{1,0:T(8,128)(2,1)S(1)}, u32[]{:S(2)}, u32[]{:S(2)}) collective-permute-start(bf16[512,128]{1,0:T(8,128)(2,1)S(1)} %convolution_convert_fusion.7), channel_id=1, source_target_pairs={{0,32},{32,64},{64,96},{96,128},{128,160},{160,192},{192,224},{224... | collective-permute-start | bytes 393224 | tf_op jit(solution)/shard_map/ppermute | solution.py:20
  14.5 89.0 %reduce-scatter.6.cloned.1.call-start = ((), (), s32[]{:S(2)}) async-start(), calls=%async_computation.4 | async-start | bytes 2359296 | tf_op jit(solution)/shard_map/reduce_scatter | solution.py:73
  18.8 13.5 %copy-start.14 = (bf16[512,128]{1,0:T(8,128)(2,1)}, bf16[512,128]{1,0:T(8,128)(2,1)S(1)}, u32[]{:S(2)}) copy-start(bf16[512,128]{1,0:T(8,128)(2,1)S(1)} %collective-permute-done) | copy-start | bytes 393220
  18.8 17.7 %copy-start.12 = (bf16[512,128]{1,0:T(8,128)(2,1)S(1)}, bf16[512,128]{1,0:T(8,128)(2,1)}, u32[]{:S(2)}) copy-start(bf16[512,128]{1,0:T(8,128)(2,1)} %copy-done.11) | copy-start | bytes 393220
  18.8 7.0 %collective-permute-start.1 = (bf16[512,128]{1,0:T(8,128)(2,1)S(1)}, bf16[512,128]{1,0:T(8,128)(2,1)S(1)}, u32[]{:S(2)}, u32[]{:S(2)}) collective-permute-start(bf16[512,128]{1,0:T(8,128)(2,1)S(1)} %collective-permute-done), channel_id=1, source_target_pairs={{0,32},{32,64},{64,96},{96,128},{128,160},{160,192},{192,224},{224... | collective-permute-start | bytes 393224 | tf_op jit(solution)/shard_map/ppermute | solution.py:20
  25.8 4.4 %collective-permute-start.2 = (bf16[512,128]{1,0:T(8,128)(2,1)S(1)}, bf16[512,128]{1,0:T(8,128)(2,1)S(1)}, u32[]{:S(2)}, u32[]{:S(2)}) collective-permute-start(bf16[512,128]{1,0:T(8,128)(2,1)S(1)} %collective-permute-done.1), channel_id=1, source_target_pairs={{0,32},{32,64},{64,96},{96,128},{128,160},{160,192},{192,224},{224... | collective-permute-start | bytes 393224 | tf_op jit(solution)/shard_map/ppermute | solution.py:20
  26.4 6.0 %copy-start.13 = (bf16[512,128]{1,0:T(8,128)(2,1)}, bf16[512,128]{1,0:T(8,128)(2,1)S(1)}, u32[]{:S(2)}) copy-start(bf16[512,128]{1,0:T(8,128)(2,1)S(1)} %collective-permute-done.4) | copy-start | bytes 393220
  26.4 3.9 collective-permute-start.5
  30.2 5.3 %collective-permute-start.3 = (bf16[512,128]{1,0:T(8,128)(2,1)S(1)}, bf16[512,128]{1,0:T(8,128)(2,1)S(1)}, u32[]{:S(2)}, u32[]{:S(2)}) collective-permute-start(bf16[512,128]{1,0:T(8,128)(2,1)S(1)} %collective-permute-done.2), channel_id=1, source_target_pairs={{0,32},{32,64},{64,96},{96,128},{128,160},{160,192},{192,224},{224... | collective-permute-start | bytes 393224 | tf_op jit(solution)/shard_map/ppermute | solution.py:20
  30.3 7.3 %collective-permute-start.6 = (bf16[512,128]{1,0:T(8,128)(2,1)S(1)}, bf16[512,128]{1,0:T(8,128)(2,1)S(1)}, u32[]{:S(2)}, u32[]{:S(2)}) collective-permute-start(bf16[512,128]{1,0:T(8,128)(2,1)S(1)} %collective-permute-done.5), channel_id=1, source_target_pairs={{32,0},{64,32},{96,64},{128,96},{160,128},{192,160},{224,192},{0,2... | collective-permute-start | bytes 393224 | tf_op jit(solution)/shard_map/ppermute | solution.py:22
  38.3 10.5 %copy-start.5 = (bf16[8,512,128]{2,1,0:T(8,128)(2,1)}, bf16[8,512,128]{2,1,0:T(8,128)(2,1)S(1)}, u32[]{:S(2)}) copy-start(bf16[8,512,128]{2,1,0:T(8,128)(2,1)S(1)} %gather_fusion) | copy-start | bytes 3145732
  46.6 2.2 copy-start.10
  53.7 3.2 copy-start.1
  65.0 2.0 copy-start.3
  69.3 93.8 %reduce-scatter.10.cloned.1.call-start = ((), (), s32[]{:S(2)}) async-start(), calls=%async_computation.6 | async-start | bytes 5898240
  103.6 3.5 copy-start.6
  107.1 3.5 copy-start.4
  122.0 1.6 copy-start.8
  122.0 274.5 %reduce-scatter.8.cloned.1.call-start = ((), (), s32[]{:S(2)}) async-start(), calls=%async_computation.5 | async-start | bytes 5406720 | tf_op jit(solution)/shard_map/reduce_scatter | solution.py:96
  123.6 5.6 %copy-start.9 = (bf16[5120,128]{1,0:T(8,128)(2,1)S(1)}, bf16[5120,128]{1,0:T(8,128)(2,1)}, u32[]{:S(2)}) copy-start(bf16[5120,128]{1,0:T(8,128)(2,1)} %param.10) | copy-start | bytes 3932164
Sparse Core Ops, SparseCore 0:
  14.7 29.2 all-gather.1
  69.4 34.1 reduce-scatter.5
  122.1 40.9 reduce-scatter.9
  167.5 229.0 reduce-scatter.7
